TPU v7x, 32 devices: a whole 2x2x4 slice. The times are simulated.
32 devices in a mesh: head: 4 (over y, x), pb: 8 (over z, core).
Axes of the slice: x: 2, y: 2, z: 4, core: 2. Of those that a mesh axis runs over, the one named last changes fastest.
Arguments:
- pair: bfloat16 [512, 512, 128], P('pb', 'head'), may hold values from -6 to 6
- tokens: bfloat16 [512, 768], P('pb'), may hold values from -6 to 6
- token_mask: int32 [512], replicated, may hold values from 0 to 1, as said below
- w_gu: bfloat16 [2, 128, 512], replicated, may hold values from -0.5 to 0.5
- w_down: bfloat16 [2, 256, 128], replicated, may hold values from -0.375 to 0.375
- w_bias: bfloat16 [128, 32], replicated, may hold values from -0.5 to 0.5
- w_q: bfloat16 [2, 768, 768], P(None, None, 'head'), may hold values from -0.21875 to 0.21875
- w_k: bfloat16 [2, 768, 768], P(None, None, 'head'), may hold values from -0.21875 to 0.21875
- w_v: bfloat16 [2, 768, 768], P(None, None, 'head'), may hold values from -0.21875 to 0.21875
- w_gate: bfloat16 [2, 768, 768], P(None, None, 'head'), may hold values from -0.21875 to 0.21875
- w_out: bfloat16 [2, 768, 768], P(None, 'head'), may hold values from -0.875 to 0.875
Outputs:
- updated: bfloat16 [512, 768], P('pb')
Inputs may be any that keep to these rules, and one draw needn't show every extreme that they name: `token_mask`: ones on a prefix of the tokens and zeros after it; at least 128 ones and at least one zero.
All inputs are finite; a program needn't handle non-finite values.
Results may differ from a plain program's by a relative error of at most 0.019.
Values may be sent and summed in bfloat16 or wider, within the bound.
A program may use at most 64 MiB of HBM per device.

v0:
```python
import math
import jax
import jax.numpy as jnp
from jax import lax
from jax.sharding import PartitionSpec as P

TRANS = 2
LAYERS = 2
HD = 48


def normalize(values):
    values = values.astype(jnp.float32)
    center = values - jnp.mean(values, axis=-1, keepdims=True)
    spread = jnp.mean(center * center, axis=-1, keepdims=True)
    return center * lax.rsqrt(spread + 1e-05)


def transition(pair_rows, w_updown, w_back):
    hidden_units = w_back.shape[0]
    normed = normalize(pair_rows).astype(jnp.bfloat16)
    mixed = jnp.dot(normed, w_updown, preferred_element_type=jnp.float32)
    hidden = (jax.nn.silu(mixed[:, :hidden_units]) * mixed[:, hidden_units:]).astype(jnp.bfloat16)
    summed = pair_rows.astype(jnp.float32) + jnp.dot(
        hidden, w_back, preferred_element_type=jnp.float32
    )
    return summed.astype(jnp.bfloat16)


def on_device(pair, tokens, token_mask, w_gu, w_down, w_bias, w_q, w_k, w_v, w_gate, w_out):
    row_count, col_count, channels = pair.shape
    entries = row_count * col_count
    block_rows = math.gcd(entries, 2048)
    blocked = pair.reshape(entries // block_rows, block_rows, channels)
    heads_all = w_bias.shape[1] // LAYERS

    def project(pair_block):
        current = pair_block
        for section_index in range(TRANS):
            current = transition(current, w_gu[section_index], w_down[section_index])
        normed = normalize(current).astype(jnp.bfloat16)
        return jnp.einsum("rc,cj->jr", normed, w_bias, preferred_element_type=jnp.float32).astype(
            jnp.bfloat16
        )

    projected = lax.map(project, blocked)
    columns_first = jnp.transpose(projected, (1, 0, 2))
    bias_local = columns_first.reshape(LAYERS, heads_all, row_count, col_count)
    layer_bias = [
        lax.all_to_all(bias_local[layer_index], "head", split_axis=0, concat_axis=2, tiled=True)
        for layer_index in range(LAYERS)
    ]
    is_real = token_mask == 1
    query_real = lax.dynamic_slice_in_dim(
        token_mask, lax.axis_index("pb") * row_count, row_count, 0
    ).astype(jnp.float32)
    local_width = w_q.shape[2]
    local_heads = local_width // HD
    scale_factor = 1.0 / HD**0.5
    state = tokens.astype(jnp.float32)
    for layer_index in range(LAYERS):
        normed = normalize(state).astype(jnp.bfloat16)
        queries = jnp.dot(normed, w_q[layer_index], preferred_element_type=jnp.float32).astype(
            jnp.bfloat16
        )
        key_proj = jnp.dot(normed, w_k[layer_index], preferred_element_type=jnp.float32).astype(
            jnp.bfloat16
        )
        value_proj = jnp.dot(normed, w_v[layer_index], preferred_element_type=jnp.float32).astype(
            jnp.bfloat16
        )
        gate_vals = jnp.dot(normed, w_gate[layer_index], preferred_element_type=jnp.float32).astype(
            jnp.bfloat16
        )
        packed = jnp.concatenate([key_proj, value_proj], axis=1)
        query_heads = queries.astype(jnp.float32).reshape(row_count, local_heads, HD)
        bias_now = layer_bias[layer_index]
        every_key = lax.all_gather(packed, "pb", axis=0, tiled=True)
        piece_len = every_key.shape[0]
        key_heads = (
            every_key[:, :local_width].astype(jnp.float32).reshape(piece_len, local_heads, HD)
        )
        value_heads = (
            every_key[:, local_width:].astype(jnp.float32).reshape(piece_len, local_heads, HD)
        )
        scores = jnp.einsum("ihd,jhd->hij", query_heads, key_heads) * scale_factor
        scores = scores + bias_now.astype(jnp.float32)
        scores = jnp.where(is_real[None, None, :], scores, -1e30)
        old_peak = jnp.full((local_heads, row_count), -1e30, jnp.float32)
        new_peak = jnp.maximum(old_peak, jnp.max(scores, axis=-1))
        exp_scores = jnp.exp(scores - new_peak[..., None])
        new_total = jnp.sum(exp_scores, axis=-1)
        new_accum = jnp.einsum("hij,jhd->hid", exp_scores, value_heads)
        finished = (new_peak, new_total, new_accum)
        final_peak, final_total, final_accum = finished
        attended = jnp.transpose(final_accum / final_total[..., None], (1, 0, 2)).reshape(
            row_count, local_width
        )
        gated = (attended * jax.nn.sigmoid(gate_vals.astype(jnp.float32))).astype(jnp.bfloat16)
        partial_out = jnp.dot(gated, w_out[layer_index], preferred_element_type=jnp.float32)
        feature_share = lax.psum_scatter(
            partial_out.astype(jnp.bfloat16), "head", scatter_dimension=1, tiled=True
        ).astype(jnp.float32)
        share_width = feature_share.shape[1]
        own_features = lax.dynamic_slice_in_dim(
            state, lax.axis_index("head") * share_width, share_width, 1
        )
        state = lax.all_gather(
            (own_features + query_real[:, None] * feature_share).astype(jnp.bfloat16),
            "head",
            axis=1,
            tiled=True,
        ).astype(jnp.float32)
    return state.astype(jnp.bfloat16)


def solution(mesh):
    placed = (
        P("pb", "head", None),
        P("pb", None),
        P(),
        P(),
        P(),
        P(),
        P(None, None, "head"),
        P(None, None, "head"),
        P(None, None, "head"),
        P(None, None, "head"),
        P(None, "head", None),
    )
    return jax.shard_map(
        on_device, mesh=mesh, in_specs=placed, out_specs=P("pb", None), check_vma=False
    )
```

profile of v0, /device:TPU:0, one launch (start us, length us, event | category | flops | bytes accessed | tf_op | source)
XLA Modules:
  0.0 150.9 jit_solution(16466473360683681310)
XLA Ops:
  6.5 22.2 %while.10 = (s32[]{:T(128)}, bf16[4,32,2048]{2,1,0:T(8,128)(2,1)S(1)}, bf16[4,2048,128]{2,1,0:T(8,128)(2,1)}, bf16[2,128,512]{2,1,0:T(8,128)(2,1)}, bf16[2,256,1...) while((s32[]{:T(128)}, bf16[4,32,2048]{2,1,0:T(8,128)(2,1)S(1)}, ...), condition=%wide.region_9.10_spmd, body=%wide.region_2.9_spmd.sunk | while | flops 836573184 | bytes 30671024 | solution.py:46
  6.5 1.1 constant_dynamic-slice_fusion.2
  7.7 0.2 copy.71
  8.2 0.7 fusion.123
  8.9 0.2 copy-done.9
  9.1 0.8 fusion.124
  10.1 0.7 fusion.125
  10.8 0.8 fusion.126
  11.8 0.2 fusion.127
  12.1 1.1 constant_dynamic-slice_fusion.2
  13.2 0.2 copy.71
  13.7 0.7 fusion.123
  14.6 0.8 fusion.124
  15.6 0.7 fusion.125
  16.4 0.8 fusion.126
  17.4 0.2 fusion.127
  17.7 1.1 constant_dynamic-slice_fusion.2
  18.8 0.2 copy.71
  19.3 0.7 fusion.123
  20.2 0.8 fusion.124
  21.2 0.7 fusion.125
  22.0 0.8 fusion.126
  23.0 0.2 fusion.127
  23.2 1.1 constant_dynamic-slice_fusion.2
  24.3 0.2 copy.71
  24.9 0.7 fusion.123
  25.8 0.8 fusion.124
  26.8 0.7 fusion.125
  27.5 0.8 fusion.126
  28.5 0.2 fusion.127
  28.8 0.2 copy.49
  29.1 0.9 squeeze.53
  29.9 5.2 %all-to-all-start = ((bf16[16,64,128]{2,1,0:T(8,128)(2,1)}), bf16[16,64,128]{2,1,0:T(8,128)(2,1)S(1)}, u32[]{:S(2)}, u32[]{:S(2)}) async-start(bf16[16,64,128]{2,1,0:T(8,128)(2,1)} %squeeze.53), calls=%async_computation | async-start | bytes 524288 | tf_op jit(solution)/shard_map/all_to_all | solution.py:50
  35.2 0.2 multiply_reduce_fusion.3
  35.5 0.2 convolution_convert_fusion.8
  35.7 0.2 convolution_convert_fusion.9
  36.1 14.7 %all_gather.12 = bf16[512,384]{1,0:T(8,128)(2,1)S(1)} all-gather(bf16[64,384]{1,0:T(8,128)(2,1)S(1)} %pad_maximum_fusion), channel_id=1, replica_groups=mesh['head'=4,'pb'=8] {'pb'}, dimensions={0}, use_global_device_ids=true | all-gather | bytes 442368 | tf_op jit(solution)/shard_map/all_gather | solution.py:78
  51.1 0.2 convolution_convert_fusion.10
  51.7 0.4 fusion.95
  52.0 0.2 fusion.55
  52.3 0.3 fusion.40
  52.7 1.5 convolution_convert_fusion.2
  54.2 0.8 copy.61
  55.0 0.2 copy.56
  55.2 0.9 squeeze.59
  56.1 4.2 %all-to-all-start.1 = ((bf16[16,64,128]{2,1,0:T(8,128)(2,1)}), bf16[16,64,128]{2,1,0:T(8,128)(2,1)S(1)}, u32[]{:S(2)}, u32[]{:S(2)}) async-start(bf16[16,64,128]{2,1,0:T(8,128)(2,1)} %squeeze.59), calls=%async_computation.1 | async-start | bytes 524288 | tf_op jit(solution)/shard_map/all_to_all | solution.py:50
  60.4 20.6 %reduce-scatter.7.cloned.1.call-done = bf16[192,64]{1,0:T(8,128)(2,1)} async-done(((bf16[768,64]{1,0:T(8,128)(2,1)}), bf16[192,64]{1,0:T(8,128)(2,1)}) %reduce-scatter.7.cloned.1.call-update) | async-done | bytes 24592
  81.0 0.9 copy.62
  82.0 8.5 %all-gather = bf16[4,192,64]{1,2,0:T(8,128)(2,1)S(1)} all-gather(bf16[1,192,64]{1,2,0:T(8,128)(2,1)S(1)} %fusion.84), channel_id=1, replica_groups=mesh['head'=4,'pb'=8] {'head'}, dimensions={0}, use_global_device_ids=true | all-gather | bytes 122880 | tf_op jit(solution)/shard_map/all_gather | solution.py:108
  90.7 0.2 reshape.143
  90.9 0.2 multiply_reduce_fusion.2
  91.2 0.2 convolution_convert_fusion.4
  91.4 0.2 convolution_convert_fusion.5
  91.8 14.5 %all_gather.14 = bf16[512,384]{1,0:T(8,128)(2,1)S(1)} all-gather(bf16[64,384]{1,0:T(8,128)(2,1)S(1)} %pad_maximum_fusion.1), channel_id=1, replica_groups=mesh['head'=4,'pb'=8] {'pb'}, dimensions={0}, use_global_device_ids=true | all-gather | bytes 442368 | tf_op jit(solution)/shard_map/all_gather | solution.py:78
  106.5 0.2 convolution_convert_fusion.6
  107.0 0.4 fusion.96
  107.4 0.2 fusion.56
  107.7 0.3 fusion.39
  108.1 0.4 convolution_convert_fusion.1
  108.5 0.8 copy.63
  109.3 24.4 %reduce-scatter.9.cloned.1.call-done = bf16[192,64]{1,0:T(8,128)(2,1)} async-done(((bf16[768,64]{1,0:T(8,128)(2,1)}), bf16[192,64]{1,0:T(8,128)(2,1)}) %reduce-scatter.9.cloned.1.call-update) | async-done | bytes 24592
  133.8 0.9 copy.64
  134.7 8.5 %all-gather.1 = bf16[4,192,64]{1,2,0:T(8,128)(2,1)S(1)} all-gather(bf16[1,192,64]{1,2,0:T(8,128)(2,1)S(1)} %fusion.85), channel_id=1, replica_groups=mesh['head'=4,'pb'=8] {'head'}, dimensions={0}, use_global_device_ids=true | all-gather | bytes 122880 | tf_op jit(solution)/shard_map/all_gather | solution.py:108
  143.3 0.8 reshape.142
  (113 shorter events, 5.0 us)
Async XLA Ops:
  6.5 1.6 %copy-start = (bf16[2,128,512]{2,1,0:T(8,128)(2,1)S(1)}, bf16[2,128,512]{2,1,0:T(8,128)(2,1)}, u32[]{:S(2)}) copy-start(bf16[2,128,512]{2,1,0:T(8,128)(2,1)} %get-tuple-element.144) | copy-start | bytes 786436 | tf_op jit(solution)/shard_map/while
  8.2 0.9 copy-start.9
  10.8 1.0 copy-start.2
  12.1 1.6 %copy-start = (bf16[2,128,512]{2,1,0:T(8,128)(2,1)S(1)}, bf16[2,128,512]{2,1,0:T(8,128)(2,1)}, u32[]{:S(2)}) copy-start(bf16[2,128,512]{2,1,0:T(8,128)(2,1)} %get-tuple-element.144) | copy-start | bytes 786436 | tf_op jit(solution)/shard_map/while
  13.7 0.9 copy-start.9
  16.4 1.0 copy-start.2
  17.6 1.6 %copy-start = (bf16[2,128,512]{2,1,0:T(8,128)(2,1)S(1)}, bf16[2,128,512]{2,1,0:T(8,128)(2,1)}, u32[]{:S(2)}) copy-start(bf16[2,128,512]{2,1,0:T(8,128)(2,1)} %get-tuple-element.144) | copy-start | bytes 786436 | tf_op jit(solution)/shard_map/while
  19.3 0.9 copy-start.9
  21.9 1.0 copy-start.2
  23.2 1.6 %copy-start = (bf16[2,128,512]{2,1,0:T(8,128)(2,1)S(1)}, bf16[2,128,512]{2,1,0:T(8,128)(2,1)}, u32[]{:S(2)}) copy-start(bf16[2,128,512]{2,1,0:T(8,128)(2,1)} %get-tuple-element.144) | copy-start | bytes 786436 | tf_op jit(solution)/shard_map/while
  24.8 0.9 copy-start.9
  27.5 1.0 copy-start.2
  28.7 6.4 %copy-start.1 = (bf16[64,768]{1,0:T(8,128)(2,1)S(1)}, bf16[64,768]{1,0:T(8,128)(2,1)}, u32[]{:S(2)}) copy-start(bf16[64,768]{1,0:T(8,128)(2,1)} %param.14) | copy-start | bytes 294916
  28.8 6.7 %copy-start.4 = (bf16[2,768,192]{1,2,0:T(8,128)(2,1)S(1)}, bf16[2,768,192]{1,2,0:T(8,128)(2,1)}, u32[]{:S(2)}) copy-start(bf16[2,768,192]{1,2,0:T(8,128)(2,1)} %param.21) | copy-start | bytes 1769476
  28.8 7.0 %copy-start.5 = (bf16[2,768,192]{1,2,0:T(8,128)(2,1)S(1)}, bf16[2,768,192]{1,2,0:T(8,128)(2,1)}, u32[]{:S(2)}) copy-start(bf16[2,768,192]{1,2,0:T(8,128)(2,1)} %param.20) | copy-start | bytes 1769476
  29.0 22.1 %copy-start.6 = (bf16[2,768,192]{1,2,0:T(8,128)(2,1)S(1)}, bf16[2,768,192]{1,2,0:T(8,128)(2,1)}, u32[]{:S(2)}) copy-start(bf16[2,768,192]{1,2,0:T(8,128)(2,1)} %param.19) | copy-start | bytes 1769476
  29.9 21.7 %all-to-all-start = ((bf16[16,64,128]{2,1,0:T(8,128)(2,1)}), bf16[16,64,128]{2,1,0:T(8,128)(2,1)S(1)}, u32[]{:S(2)}, u32[]{:S(2)}) async-start(bf16[16,64,128]{2,1,0:T(8,128)(2,1)} %squeeze.53), calls=%async_computation | async-start | bytes 524288 | tf_op jit(solution)/shard_map/all_to_all | solution.py:50
  35.1 45.9 %reduce-scatter.7.cloned.1.call-start = ((), (), s32[]{:S(2)}) async-start(), calls=%async_computation.4 | async-start | bytes 245760
  35.5 16.2 %copy-start.3 = (s32[512]{0:T(512)S(1)}, s32[512]{0:T(512)}, u32[]{:S(2)}) copy-start(s32[512]{0:T(512)} %param.15) | copy-start | bytes 6148
  56.1 51.0 %all-to-all-start.1 = ((bf16[16,64,128]{2,1,0:T(8,128)(2,1)}), bf16[16,64,128]{2,1,0:T(8,128)(2,1)S(1)}, u32[]{:S(2)}, u32[]{:S(2)}) async-start(bf16[16,64,128]{2,1,0:T(8,128)(2,1)} %squeeze.59), calls=%async_computation.1 | async-start | bytes 524288 | tf_op jit(solution)/shard_map/all_to_all | solution.py:50
  60.3 73.5 %reduce-scatter.9.cloned.1.call-start = ((), (), s32[]{:S(2)}) async-start(), calls=%async_computation.5 | async-start | bytes 245760
  106.4 1.7 %copy-start.7 = (bf16[2,192,768]{2,1,0:T(8,128)(2,1)S(1)}, bf16[2,192,768]{2,1,0:T(8,128)(2,1)}, u32[]{:S(2)}) copy-start(bf16[2,192,768]{2,1,0:T(8,128)(2,1)} %param.23) | copy-start | bytes 1769476
  106.4 1.7 %copy-start.8 = (bf16[2,768,192]{1,2,0:T(8,128)(2,1)S(1)}, bf16[2,768,192]{1,2,0:T(8,128)(2,1)}, u32[]{:S(2)}) copy-start(bf16[2,768,192]{1,2,0:T(8,128)(2,1)} %param.22) | copy-start | bytes 1769476
Sparse Core Ops, SparseCore 0:
  55.1 25.8 reduce-scatter.6
  109.5 24.2 reduce-scatter.8
where the time goes:
time: 152 us; the launch traced here: 151 us
  blocking collectives  46.2 us (30%)
  waiting for transfers between devices  45.1 us (30%)
  matrix products  18.1 us (12%)
  local copies, waits for them, and re-layouts  14 us (9%)
  between operations  13.9 us (9%)
  starting transfers between devices  9.39 us (6%)
  other arithmetic  3.75 us (2%)
    unnamed x4, waiting for transfers between devices  45.1 us
    all_gather x2, blocking collectives, on_device(): every_key = lax.all_gather(packed, 'pb', axis=0, tiled=True)  29.2 us
    all_gather x2, blocking collectives, on_device(): lax.all_gather((own_features + query_real[:, None] * feature_share).astyp...  17 us
    all_to_all x2, starting transfers between devices, on_device(): lax.all_to_all(bias_local[layer_index], 'head', split_axis=0, concat_axis...  9.39 us
    dot_general x8, matrix products, transition(): jnp.dot(hidden, w_back, preferred_element_type=jnp.float32)  6.65 us
    dot_general x8, matrix products, transition(): mixed = jnp.dot(normed, w_updown, preferred_element_type=jnp.float32)  5.9 us
    dynamic_slice x8, local copies, waits for them, and re-layouts, on_device(): projected = lax.map(project, blocked)  5.33 us
    unnamed x19, local copies, waits for them, and re-layouts  4.22 us
  transfers between devices with their start and end apart: 4, of which 2 were waited for; matrix products, arithmetic and copies ran while one was open for 4% of the time, Pallas kernels for 0%

commit v1 on v0

--- a/solution.py
+++ b/solution.py
@@ -7,6 +7,16 @@
 TRANS = 2
 LAYERS = 2
 HD = 48
+
+
+def turned_line(block, mesh_axis, along):
+    size = lax.axis_size(mesh_axis)
+    held, blocks = (block, [block])
+    for _ in range(size - 1):
+        held = lax.ppermute(held, mesh_axis, [(i, (i + 1) % size) for i in range(size)])
+        blocks.insert(0, held)
+    line = jnp.concatenate(blocks, axis=along)
+    return jnp.roll(line, (lax.axis_index(mesh_axis) + 1) * block.shape[along], axis=along)
 
 
 def normalize(values):
@@ -75,7 +85,7 @@
         packed = jnp.concatenate([key_proj, value_proj], axis=1)
         query_heads = queries.astype(jnp.float32).reshape(row_count, local_heads, HD)
         bias_now = layer_bias[layer_index]
-        every_key = lax.all_gather(packed, "pb", axis=0, tiled=True)
+        every_key = turned_line(packed, "pb", 0)
         piece_len = every_key.shape[0]
         key_heads = (
             every_key[:, :local_width].astype(jnp.float32).reshape(piece_len, local_heads, HD)

time: 152 us -> 185 us (1.22)
  waiting for transfers between devices: 45.1 us -> 104 us
  blocking collectives: 46.2 us -> 17 us
  other arithmetic: 3.75 us -> 7.17 us
    ppermute x0 -> x14, waiting for transfers between devices: none -> 58.9 us  [turned_line(): lax.ppermute(held, mesh_axis, [(i, (i + 1) % size) for i in range(size)])]
    all_gather x2 -> x0, blocking collectives: 29.2 us -> none  [on_device(): every_key = lax.all_gather(packed, 'pb', axis=0, tiled=True)]
    unnamed x19 -> x35, local copies, waits for them, and re-layouts: 4.22 us -> 4.38 us
  transfers between devices with their start and end apart: 4 -> 18, of which waited for: 2 -> 14; matrix products, arithmetic and copies ran while one was open for 4% -> 14% of each run, Pallas kernels for 0% -> 0%
where the time goes in v1:
time: 185 us; the launch traced here: 184 us
  waiting for transfers between devices  104 us (56%)
  matrix products  18.9 us (10%)
  blocking collectives  17 us (9%)
  local copies, waits for them, and re-layouts  14.2 us (8%)
  between operations  14 us (8%)
  starting transfers between devices  8.36 us (5%)
  other arithmetic  7.17 us (4%)
    ppermute x14, waiting for transfers between devices, turned_line(): lax.ppermute(held, mesh_axis, [(i, (i + 1) % size) for i in range(size)])  58.9 us
    unnamed x4, waiting for transfers between devices  45.2 us
    all_gather x2, blocking collectives, on_device(): lax.all_gather((own_features + query_real[:, None] * feature_share).astyp...  17 us
    all_to_all x2, starting transfers between devices, on_device(): lax.all_to_all(bias_local[layer_index], 'head', split_axis=0, concat_axis...  7.6 us
    dot_general x8, matrix products, transition(): jnp.dot(hidden, w_back, preferred_element_type=jnp.float32)  6.51 us
    dot_general x8, matrix products, transition(): mixed = jnp.dot(normed, w_updown, preferred_element_type=jnp.float32)  5.88 us
    dynamic_slice x8, local copies, waits for them, and re-layouts, on_device(): projected = lax.map(project, blocked)  5.36 us
    unnamed x35, local copies, waits for them, and re-layouts  4.38 us
  transfers between devices with their start and end apart: 18, of which 14 were waited for; matrix products, arithmetic and copies ran while one was open for 14% of the time, Pallas kernels for 0%

profile of v1, /device:TPU:0, one launch (start us, length us, event | category | flops | bytes accessed | tf_op | source)
XLA Modules:
  0.0 184.3 jit_solution(10783967497559082110)
XLA Ops:
  6.5 1.0 convert_reduce_fusion.1
  7.6 1.1 multiply_reduce_fusion.3
  8.7 1.3 convolution_convert_fusion.8
  9.9 1.3 convolution_convert_fusion.9
  11.3 0.5 collective-permute-start
  11.8 5.8 %collective-permute-done = bf16[64,384]{1,0:T(8,128)(2,1)S(1)} collective-permute-done((bf16[64,384]{1,0:T(8,128)(2,1)S(1)}, bf16[64,384]{1,0:T(8,128)(2,1)S(1)}, u32[]{:S(2)}, u32[]{:S(2)}) %collective-permute-start) | collective-permute-done | bytes 49184 | tf_op jit(solution)/shard_map/ppermute | solution.py:16
  17.6 5.3 %collective-permute-done.1 = bf16[64,384]{1,0:T(8,128)(2,1)S(1)} collective-permute-done((bf16[64,384]{1,0:T(8,128)(2,1)S(1)}, bf16[64,384]{1,0:T(8,128)(2,1)S(1)}, u32[]{:S(2)}, u32[]{:S(2)}) %collective-permute-start.1) | collective-permute-done | bytes 49184 | tf_op jit(solution)/shard_map/ppermute | solution.py:16
  23.0 5.3 %collective-permute-done.2 = bf16[64,384]{1,0:T(8,128)(2,1)S(1)} collective-permute-done((bf16[64,384]{1,0:T(8,128)(2,1)S(1)}, bf16[64,384]{1,0:T(8,128)(2,1)S(1)}, u32[]{:S(2)}, u32[]{:S(2)}) %collective-permute-start.2) | collective-permute-done | bytes 49184 | tf_op jit(solution)/shard_map/ppermute | solution.py:16
  28.3 22.1 %while.10 = (s32[]{:T(128)}, bf16[4,32,2048]{2,1,0:T(8,128)(2,1)S(1)}, bf16[4,2048,128]{2,1,0:T(8,128)(2,1)}, bf16[2,128,512]{2,1,0:T(8,128)(2,1)}, bf16[2,256,1...) while((s32[]{:T(128)}, bf16[4,32,2048]{2,1,0:T(8,128)(2,1)S(1)}, ...), condition=%wide.region_9.11_spmd, body=%wide.region_2.10_spmd.sunk | while | flops 836573184 | bytes 30671024 | solution.py:56
  28.3 1.1 constant_dynamic-slice_fusion.2
  29.9 0.7 fusion.125
  30.8 0.8 fusion.126
  31.8 0.7 fusion.127
  32.5 0.8 fusion.128
  33.5 0.2 fusion.129
  33.8 1.1 constant_dynamic-slice_fusion.2
  35.4 0.7 fusion.125
  36.3 0.8 fusion.126
  37.3 0.7 fusion.127
  38.1 0.8 fusion.128
  39.0 0.2 fusion.129
  39.3 1.1 constant_dynamic-slice_fusion.2
  41.0 0.7 fusion.125
  41.9 0.8 fusion.126
  42.8 0.7 fusion.127
  43.6 0.8 fusion.128
  44.6 0.2 fusion.129
  44.8 1.1 constant_dynamic-slice_fusion.2
  46.5 0.7 fusion.125
  47.4 0.8 fusion.126
  48.4 0.7 fusion.127
  49.1 0.8 fusion.128
  50.1 0.2 fusion.129
  50.7 0.9 squeeze.53
  51.6 4.2 %all-to-all-start = ((bf16[16,64,128]{2,1,0:T(8,128)(2,1)}), bf16[16,64,128]{2,1,0:T(8,128)(2,1)S(1)}, u32[]{:S(2)}, u32[]{:S(2)}) async-start(bf16[16,64,128]{2,1,0:T(8,128)(2,1)} %squeeze.53), calls=%async_computation | async-start | bytes 524288 | tf_op jit(solution)/shard_map/all_to_all | solution.py:60
  56.1 5.0 %collective-permute-done.5 = bf16[64,384]{1,0:T(8,128)(2,1)S(1)} collective-permute-done((bf16[64,384]{1,0:T(8,128)(2,1)S(1)}, bf16[64,384]{1,0:T(8,128)(2,1)S(1)}, u32[]{:S(2)}, u32[]{:S(2)}) %collective-permute-start.5) | collective-permute-done | bytes 49184 | tf_op jit(solution)/shard_map/ppermute | solution.py:16
  61.3 5.2 %collective-permute-done.6 = bf16[64,384]{1,0:T(8,128)(2,1)S(1)} collective-permute-done((bf16[64,384]{1,0:T(8,128)(2,1)S(1)}, bf16[64,384]{1,0:T(8,128)(2,1)S(1)}, u32[]{:S(2)}, u32[]{:S(2)}) %collective-permute-start.6) | collective-permute-done | bytes 49184 | tf_op jit(solution)/shard_map/ppermute | solution.py:16
  66.6 0.7 fusion.58
  67.8 0.4 fusion.97
  68.4 0.3 fusion.40
  68.9 0.5 convolution_convert_fusion.2
  69.3 0.8 copy.61
  70.3 23.0 %reduce-scatter.7.cloned.1.call-done = bf16[192,64]{1,0:T(8,128)(2,1)} async-done(((bf16[768,64]{1,0:T(8,128)(2,1)}), bf16[192,64]{1,0:T(8,128)(2,1)}) %reduce-scatter.7.cloned.1.call-update) | async-done | bytes 24592
  93.2 0.9 copy.62
  94.2 8.5 %all-gather = bf16[4,192,64]{1,2,0:T(8,128)(2,1)S(1)} all-gather(bf16[1,192,64]{1,2,0:T(8,128)(2,1)S(1)} %fusion.86), channel_id=1, replica_groups=mesh['head'=4,'pb'=8] {'head'}, dimensions={0}, use_global_device_ids=true | all-gather | bytes 122880 | tf_op jit(solution)/shard_map/all_gather | solution.py:118
  104.0 5.3 %collective-permute-done.7 = bf16[64,384]{1,0:T(8,128)(2,1)S(1)} collective-permute-done((bf16[64,384]{1,0:T(8,128)(2,1)S(1)}, bf16[64,384]{1,0:T(8,128)(2,1)S(1)}, u32[]{:S(2)}, u32[]{:S(2)}) %collective-permute-start.7) | collective-permute-done | bytes 49184 | tf_op jit(solution)/shard_map/ppermute | solution.py:16
  109.3 5.3 %collective-permute-done.8 = bf16[64,384]{1,0:T(8,128)(2,1)S(1)} collective-permute-done((bf16[64,384]{1,0:T(8,128)(2,1)S(1)}, bf16[64,384]{1,0:T(8,128)(2,1)S(1)}, u32[]{:S(2)}, u32[]{:S(2)}) %collective-permute-start.8) | collective-permute-done | bytes 49184 | tf_op jit(solution)/shard_map/ppermute | solution.py:16
  114.7 5.3 %collective-permute-done.9 = bf16[64,384]{1,0:T(8,128)(2,1)S(1)} collective-permute-done((bf16[64,384]{1,0:T(8,128)(2,1)S(1)}, bf16[64,384]{1,0:T(8,128)(2,1)S(1)}, u32[]{:S(2)}, u32[]{:S(2)}) %collective-permute-start.9) | collective-permute-done | bytes 49184 | tf_op jit(solution)/shard_map/ppermute | solution.py:16
  120.0 5.3 %collective-permute-done.10 = bf16[64,384]{1,0:T(8,128)(2,1)S(1)} collective-permute-done((bf16[64,384]{1,0:T(8,128)(2,1)S(1)}, bf16[64,384]{1,0:T(8,128)(2,1)S(1)}, u32[]{:S(2)}, u32[]{:S(2)}) %collective-permute-start.10) | collective-permute-done | bytes 49184 | tf_op jit(solution)/shard_map/ppermute | solution.py:16
  125.3 5.3 %collective-permute-done.11 = bf16[64,384]{1,0:T(8,128)(2,1)S(1)} collective-permute-done((bf16[64,384]{1,0:T(8,128)(2,1)S(1)}, bf16[64,384]{1,0:T(8,128)(2,1)S(1)}, u32[]{:S(2)}, u32[]{:S(2)}) %collective-permute-start.11) | collective-permute-done | bytes 49184 | tf_op jit(solution)/shard_map/ppermute | solution.py:16
  130.8 0.9 squeeze.59
  131.7 3.4 %all-to-all-start.1 = ((bf16[16,64,128]{2,1,0:T(8,128)(2,1)}), bf16[16,64,128]{2,1,0:T(8,128)(2,1)S(1)}, u32[]{:S(2)}, u32[]{:S(2)}) async-start(bf16[16,64,128]{2,1,0:T(8,128)(2,1)} %squeeze.59), calls=%async_computation.1 | async-start | bytes 524288 | tf_op jit(solution)/shard_map/all_to_all | solution.py:60
  135.1 0.8 collective-permute-done.12
  136.3 5.0 %collective-permute-done.13 = bf16[64,384]{1,0:T(8,128)(2,1)S(1)} collective-permute-done((bf16[64,384]{1,0:T(8,128)(2,1)S(1)}, bf16[64,384]{1,0:T(8,128)(2,1)S(1)}, u32[]{:S(2)}, u32[]{:S(2)}) %collective-permute-start.13) | collective-permute-done | bytes 49184 | tf_op jit(solution)/shard_map/ppermute | solution.py:16
  141.4 0.7 fusion.57
  142.6 0.4 fusion.98
  143.0 0.2 fusion.56
  143.2 0.3 fusion.39
  143.6 0.4 convolution_convert_fusion.1
  144.0 0.8 copy.63
  144.9 22.3 %reduce-scatter.9.cloned.1.call-done = bf16[192,64]{1,0:T(8,128)(2,1)} async-done(((bf16[768,64]{1,0:T(8,128)(2,1)}), bf16[192,64]{1,0:T(8,128)(2,1)}) %reduce-scatter.9.cloned.1.call-update) | async-done | bytes 24592
  167.1 0.9 copy.64
  168.1 8.5 %all-gather.1 = bf16[4,192,64]{1,2,0:T(8,128)(2,1)S(1)} all-gather(bf16[1,192,64]{1,2,0:T(8,128)(2,1)S(1)} %fusion.87), channel_id=1, replica_groups=mesh['head'=4,'pb'=8] {'head'}, dimensions={0}, use_global_device_ids=true | all-gather | bytes 122880 | tf_op jit(solution)/shard_map/all_gather | solution.py:118
  176.7 0.8 reshape.142
  (159 shorter events, 8.3 us)
Async XLA Ops:
  11.3 6.3 %collective-permute-start = (bf16[64,384]{1,0:T(8,128)(2,1)S(1)}, bf16[64,384]{1,0:T(8,128)(2,1)S(1)}, u32[]{:S(2)}, u32[]{:S(2)}) collective-permute-start(bf16[64,384]{1,0:T(8,128)(2,1)S(1)} %pad_maximum_fusion), channel_id=1, source_target_pairs={{0,1},{1,2},{2,3},{3,4},{4,5},{5,6},{6,7},{7,0},{8,9},{9,10},{10,1... | collective-permute-start | bytes 147464 | tf_op jit(solution)/shard_map/ppermute | solution.py:16
  17.6 5.3 %collective-permute-start.1 = (bf16[64,384]{1,0:T(8,128)(2,1)S(1)}, bf16[64,384]{1,0:T(8,128)(2,1)S(1)}, u32[]{:S(2)}, u32[]{:S(2)}) collective-permute-start(bf16[64,384]{1,0:T(8,128)(2,1)S(1)} %collective-permute-done), channel_id=1, source_target_pairs={{0,1},{1,2},{2,3},{3,4},{4,5},{5,6},{6,7},{7,0},{8,9},{9,10},{10,1... | collective-permute-start | bytes 147464 | tf_op jit(solution)/shard_map/ppermute | solution.py:16
  22.9 5.3 %collective-permute-start.2 = (bf16[64,384]{1,0:T(8,128)(2,1)S(1)}, bf16[64,384]{1,0:T(8,128)(2,1)S(1)}, u32[]{:S(2)}, u32[]{:S(2)}) collective-permute-start(bf16[64,384]{1,0:T(8,128)(2,1)S(1)} %collective-permute-done.1), channel_id=1, source_target_pairs={{0,1},{1,2},{2,3},{3,4},{4,5},{5,6},{6,7},{7,0},{8,9},{9,10},{10,1... | collective-permute-start | bytes 147464 | tf_op jit(solution)/shard_map/ppermute | solution.py:16
  28.3 22.1 %collective-permute-start.3 = (bf16[64,384]{1,0:T(8,128)(2,1)S(1)}, bf16[64,384]{1,0:T(8,128)(2,1)S(1)}, u32[]{:S(2)}, u32[]{:S(2)}) collective-permute-start(bf16[64,384]{1,0:T(8,128)(2,1)S(1)} %collective-permute-done.2), channel_id=1, source_target_pairs={{0,1},{1,2},{2,3},{3,4},{4,5},{5,6},{6,7},{7,0},{8,9},{9,10},{10,1... | collective-permute-start | bytes 147464 | tf_op jit(solution)/shard_map/ppermute | solution.py:16
  28.3 1.6 copy-start
  29.9 0.9 copy-start.10
  32.5 1.0 copy-start.2
  33.8 1.6 copy-start
  35.4 0.9 copy-start.10
  38.1 1.0 copy-start.2
  39.3 1.6 copy-start
  40.9 0.9 copy-start.10
  43.6 1.0 copy-start.2
  44.8 1.6 copy-start
  46.5 0.9 copy-start.10
  49.1 1.0 copy-start.2
  50.3 5.5 %copy-start.1 = (bf16[64,768]{1,0:T(8,128)(2,1)S(1)}, bf16[64,768]{1,0:T(8,128)(2,1)}, u32[]{:S(2)}) copy-start(bf16[64,768]{1,0:T(8,128)(2,1)} %param.16) | copy-start | bytes 294916
  50.3 5.5 %copy-start.6 = (bf16[2,768,192]{1,2,0:T(8,128)(2,1)S(1)}, bf16[2,768,192]{1,2,0:T(8,128)(2,1)}, u32[]{:S(2)}) copy-start(bf16[2,768,192]{1,2,0:T(8,128)(2,1)} %param.21) | copy-start | bytes 1769476
  50.4 10.8 %copy-start.3 = (s32[512]{0:T(512)S(1)}, s32[512]{0:T(512)}, u32[]{:S(2)}) copy-start(s32[512]{0:T(512)} %param.17) | copy-start | bytes 6148
  50.4 5.4 %collective-permute-start.4 = (bf16[64,384]{1,0:T(8,128)(2,1)S(1)}, bf16[64,384]{1,0:T(8,128)(2,1)S(1)}, u32[]{:S(2)}, u32[]{:S(2)}) collective-permute-start(bf16[64,384]{1,0:T(8,128)(2,1)S(1)} %collective-permute-done.3), channel_id=1, source_target_pairs={{0,1},{1,2},{2,3},{3,4},{4,5},{5,6},{6,7},{7,0},{8,9},{9,10},{10,1... | collective-permute-start | bytes 147464 | tf_op jit(solution)/shard_map/ppermute | solution.py:16
  51.6 16.3 %all-to-all-start = ((bf16[16,64,128]{2,1,0:T(8,128)(2,1)}), bf16[16,64,128]{2,1,0:T(8,128)(2,1)S(1)}, u32[]{:S(2)}, u32[]{:S(2)}) async-start(bf16[16,64,128]{2,1,0:T(8,128)(2,1)} %squeeze.53), calls=%async_computation | async-start | bytes 524288 | tf_op jit(solution)/shard_map/all_to_all | solution.py:60
  55.8 37.5 %reduce-scatter.7.cloned.1.call-start = ((), (), s32[]{:S(2)}) async-start(), calls=%async_computation.4 | async-start | bytes 245760
  55.8 5.4 %collective-permute-start.5 = (bf16[64,384]{1,0:T(8,128)(2,1)S(1)}, bf16[64,384]{1,0:T(8,128)(2,1)S(1)}, u32[]{:S(2)}, u32[]{:S(2)}) collective-permute-start(bf16[64,384]{1,0:T(8,128)(2,1)S(1)} %collective-permute-done.4), channel_id=1, source_target_pairs={{0,1},{1,2},{2,3},{3,4},{4,5},{5,6},{6,7},{7,0},{8,9},{9,10},{10,1... | collective-permute-start | bytes 147464 | tf_op jit(solution)/shard_map/ppermute | solution.py:16
  61.1 5.3 %collective-permute-start.6 = (bf16[64,384]{1,0:T(8,128)(2,1)S(1)}, bf16[64,384]{1,0:T(8,128)(2,1)S(1)}, u32[]{:S(2)}, u32[]{:S(2)}) collective-permute-start(bf16[64,384]{1,0:T(8,128)(2,1)S(1)} %collective-permute-done.5), channel_id=1, source_target_pairs={{0,1},{1,2},{2,3},{3,4},{4,5},{5,6},{6,7},{7,0},{8,9},{9,10},{10,1... | collective-permute-start | bytes 147464 | tf_op jit(solution)/shard_map/ppermute | solution.py:16
  67.4 1.5 copy-start.7
  67.4 1.5 copy-start.8
  68.8 34.7 %copy-start.4 = (bf16[2,768,192]{1,2,0:T(8,128)(2,1)S(1)}, bf16[2,768,192]{1,2,0:T(8,128)(2,1)}, u32[]{:S(2)}) copy-start(bf16[2,768,192]{1,2,0:T(8,128)(2,1)} %param.23) | copy-start | bytes 1769476
  68.9 34.8 %copy-start.5 = (bf16[2,768,192]{1,2,0:T(8,128)(2,1)S(1)}, bf16[2,768,192]{1,2,0:T(8,128)(2,1)}, u32[]{:S(2)}) copy-start(bf16[2,768,192]{1,2,0:T(8,128)(2,1)} %param.22) | copy-start | bytes 1769476
  104.0 5.3 %collective-permute-start.7 = (bf16[64,384]{1,0:T(8,128)(2,1)S(1)}, bf16[64,384]{1,0:T(8,128)(2,1)S(1)}, u32[]{:S(2)}, u32[]{:S(2)}) collective-permute-start(bf16[64,384]{1,0:T(8,128)(2,1)S(1)} %pad_maximum_fusion.1), channel_id=1, source_target_pairs={{0,1},{1,2},{2,3},{3,4},{4,5},{5,6},{6,7},{7,0},{8,9},{9,10},{10,1... | collective-permute-start | bytes 147464 | tf_op jit(solution)/shard_map/ppermute | solution.py:16
  109.3 5.3 %collective-permute-start.8 = (bf16[64,384]{1,0:T(8,128)(2,1)S(1)}, bf16[64,384]{1,0:T(8,128)(2,1)S(1)}, u32[]{:S(2)}, u32[]{:S(2)}) collective-permute-start(bf16[64,384]{1,0:T(8,128)(2,1)S(1)} %collective-permute-done.7), channel_id=1, source_target_pairs={{0,1},{1,2},{2,3},{3,4},{4,5},{5,6},{6,7},{7,0},{8,9},{9,10},{10,1... | collective-permute-start | bytes 147464 | tf_op jit(solution)/shard_map/ppermute | solution.py:16
  114.7 5.3 %collective-permute-start.9 = (bf16[64,384]{1,0:T(8,128)(2,1)S(1)}, bf16[64,384]{1,0:T(8,128)(2,1)S(1)}, u32[]{:S(2)}, u32[]{:S(2)}) collective-permute-start(bf16[64,384]{1,0:T(8,128)(2,1)S(1)} %collective-permute-done.8), channel_id=1, source_target_pairs={{0,1},{1,2},{2,3},{3,4},{4,5},{5,6},{6,7},{7,0},{8,9},{9,10},{10,1... | collective-permute-start | bytes 147464 | tf_op jit(solution)/shard_map/ppermute | solution.py:16
  120.0 5.3 %collective-permute-start.10 = (bf16[64,384]{1,0:T(8,128)(2,1)S(1)}, bf16[64,384]{1,0:T(8,128)(2,1)S(1)}, u32[]{:S(2)}, u32[]{:S(2)}) collective-permute-start(bf16[64,384]{1,0:T(8,128)(2,1)S(1)} %collective-permute-done.9), channel_id=1, source_target_pairs={{0,1},{1,2},{2,3},{3,4},{4,5},{5,6},{6,7},{7,0},{8,9},{9,10},{10,1... | collective-permute-start | bytes 147464 | tf_op jit(solution)/shard_map/ppermute | solution.py:16
  125.3 5.3 %collective-permute-start.11 = (bf16[64,384]{1,0:T(8,128)(2,1)S(1)}, bf16[64,384]{1,0:T(8,128)(2,1)S(1)}, u32[]{:S(2)}, u32[]{:S(2)}) collective-permute-start(bf16[64,384]{1,0:T(8,128)(2,1)S(1)} %collective-permute-done.10), channel_id=1, source_target_pairs={{0,1},{1,2},{2,3},{3,4},{4,5},{5,6},{6,7},{7,0},{8,9},{9,10},{10,1... | collective-permute-start | bytes 147464 | tf_op jit(solution)/shard_map/ppermute | solution.py:16
  130.6 5.3 %collective-permute-start.12 = (bf16[64,384]{1,0:T(8,128)(2,1)S(1)}, bf16[64,384]{1,0:T(8,128)(2,1)S(1)}, u32[]{:S(2)}, u32[]{:S(2)}) collective-permute-start(bf16[64,384]{1,0:T(8,128)(2,1)S(1)} %collective-permute-done.11), channel_id=1, source_target_pairs={{0,1},{1,2},{2,3},{3,4},{4,5},{5,6},{6,7},{7,0},{8,9},{9,10},{10,1... | collective-permute-start | bytes 147464 | tf_op jit(solution)/shard_map/ppermute | solution.py:16
  131.7 10.9 %all-to-all-start.1 = ((bf16[16,64,128]{2,1,0:T(8,128)(2,1)}), bf16[16,64,128]{2,1,0:T(8,128)(2,1)S(1)}, u32[]{:S(2)}, u32[]{:S(2)}) async-start(bf16[16,64,128]{2,1,0:T(8,128)(2,1)} %squeeze.59), calls=%async_computation.1 | async-start | bytes 524288 | tf_op jit(solution)/shard_map/all_to_all | solution.py:60
  135.1 32.0 %reduce-scatter.9.cloned.1.call-start = ((), (), s32[]{:S(2)}) async-start(), calls=%async_computation.5 | async-start | bytes 245760
  135.9 5.3 %collective-permute-start.13 = (bf16[64,384]{1,0:T(8,128)(2,1)S(1)}, bf16[64,384]{1,0:T(8,128)(2,1)S(1)}, u32[]{:S(2)}, u32[]{:S(2)}) collective-permute-start(bf16[64,384]{1,0:T(8,128)(2,1)S(1)} %collective-permute-done.12), channel_id=1, source_target_pairs={{0,1},{1,2},{2,3},{3,4},{4,5},{5,6},{6,7},{7,0},{8,9},{9,10},{10,1... | collective-permute-start | bytes 147464 | tf_op jit(solution)/shard_map/ppermute | solution.py:16
  142.2 1.4 copy-start.9
Sparse Core Ops, SparseCore 0:
  70.3 22.8 reduce-scatter.6
  145.0 22.0 reduce-scatter.8
